TPU v7x, 32 devices: a whole 2x2x4 slice. The times are simulated.
32 devices in a mesh: seq: 2 (over core), depth: 2 (over x), vocab: 8 (over z, y).
Axes of the slice: x: 2, y: 2, z: 4, core: 2. Of those that a mesh axis runs over, the one named last changes fastest.
Arguments:
- hidden: bfloat16 [2, 128, 7168], P('depth', ('seq', 'vocab')), may hold values from -24 to 24
- embedding: bfloat16 [16160, 7168], P(('seq', 'vocab')), may hold values from -1 to 1
- targets: int32 [2, 128], P('depth', ('seq', 'vocab')), may hold values from 0 to 16159
- mask: int32 [2, 128], P('depth', ('seq', 'vocab')), may hold values 0 or 1
Outputs:
- nll: float32 [2, 128], P('depth', ('seq', 'vocab'))
- loss: float32 [], replicated
- grad_norm: float32 [], replicated
All inputs are finite; a program needn't handle non-finite values. No bound on the sum of `mask` on one device may be relied on, other than what follows from the above.
Results may differ from a plain program's by a relative error of at most 0.0023.
Values may be sent and summed in bfloat16 or wider, within the bound.
No kernel may reach another device: no remote copies, remote signals or barrier semaphores. Data moves between devices by JAX's collectives and lax.ppermute only.
A program may use at most 128 MiB of HBM per device.

v0:
```python
import jax
import jax.numpy as jnp
from jax import lax
from jax.sharding import PartitionSpec as P


def swapped(value, axis, apart):
    mask = 2**apart
    pairs = [(source, source ^ mask) for source in range(lax.axis_size(axis))]
    return lax.ppermute(value, axis, pairs)


def rows_product(grad_rows, states):
    part = lax.dot_general(
        grad_rows, states, (((0,), (0,)), ((), ())), preferred_element_type=jnp.float32
    )
    return part


def local(hidden, embedding, targets, mask):
    states, picks, flags = (
        lax.all_gather(hidden, ("seq", "vocab"), axis=1, tiled=True),
        lax.all_gather(targets, ("seq", "vocab"), axis=1, tiled=True),
        lax.all_gather(mask, ("seq", "vocab"), axis=1, tiled=True),
    )
    states = states[0]
    picks = picks[0]
    live = flags[0].astype(jnp.float32)
    width = embedding.shape[0]
    offset = lax.axis_index(("seq", "vocab")) * width
    logits = lax.dot_general(
        states, embedding, (((1,), (1,)), ((), ())), preferred_element_type=jnp.float32
    )
    ids = offset + lax.broadcasted_iota(jnp.int32, (1, width), 1)
    onehot = picks[:, None] == ids
    local_peak = jnp.max(logits, axis=1)
    chosen = jnp.sum(jnp.where(onehot, logits, jnp.zeros((), jnp.float32)), axis=1)
    peak = lax.pmax(local_peak, ("seq", "vocab"))
    total, target = lax.psum(
        (jnp.sum(jnp.exp(logits - peak[:, None]), axis=1), chosen), ("seq", "vocab")
    )
    lse = peak + jnp.log(total)
    nll = lse - target
    side = lax.axis_index("depth")
    weight = jnp.where(side == 0, jnp.float32(1.0), jnp.float32(0.3))
    coef = weight / jnp.maximum(jnp.sum(live), jnp.float32(1.0))
    loss = lax.psum(coef * jnp.sum(live * nll), "depth")
    grad_rows = (
        coef * live[:, None] * (jnp.exp(logits - lse[:, None]) - onehot.astype(jnp.float32))
    ).astype(jnp.bfloat16)
    half = width // 2
    mine = lax.dynamic_slice_in_dim(grad_rows, side * half, half, 1)
    other = lax.dynamic_slice_in_dim(grad_rows, (1 - side) * half, half, 1)
    recv_grad, recv_states = swapped((other, states), "depth", 0)
    own_part = rows_product(mine, states).astype(jnp.bfloat16)
    peer_part = rows_product(recv_grad, recv_states).astype(jnp.bfloat16)
    own_part, peer_part = lax.optimization_barrier((own_part, peer_part))
    summed = own_part.astype(jnp.float32) + peer_part.astype(jnp.float32)
    square = jnp.sum(summed * summed)
    grad_norm = jnp.sqrt(lax.psum(square, ("seq", "depth", "vocab")))
    count = hidden.shape[1]
    start = lax.axis_index(("seq", "vocab")) * count
    nll_own = lax.dynamic_slice_in_dim(nll, start, count, 0)[None, :]
    return (nll_own, loss, grad_norm)


def solution(mesh):
    placed = (
        P("depth", ("seq", "vocab"), None),
        P(("seq", "vocab"), None),
        P("depth", ("seq", "vocab")),
        P("depth", ("seq", "vocab")),
    )
    return jax.shard_map(
        local,
        mesh=mesh,
        in_specs=placed,
        out_specs=(P("depth", ("seq", "vocab")), P(), P()),
        check_vma=False,
    )
```

profile of v0, /device:TPU:12, one launch (start us, length us, event | category | flops | bytes accessed | tf_op | source)
XLA Modules:
  0.0 202.1 jit_solution(6596375111063482655)
XLA Ops:
  7.2 0.0 all-gather.2.cloned.1.call-start
  7.2 0.7 all-gather.2.cloned.1.call-update
  7.9 1.2 dynamic-slice
  9.8 0.8 bitcast_dynamic-update-slice_fusion.1
  10.6 0.7 bitcast_dynamic-update-slice_fusion
  11.3 11.3 %all-reduce.2 = (s32[128]{0:T(128)S(1)}, s32[128]{0:T(128)S(1)}) all-reduce(s32[128]{0:T(128)S(1)} %bitcast_dynamic-update-slice_fusion.1, s32[128]{0:T(128)S(1)} %bitcast_dynamic-update-slice_fusion), channel_id=1, replica_groups=mesh['seq'=2,'depth'=2,'vocab'=8] {'seq','vocab'}, use_global_device_ids=true, to_apply=%add | all-reduce | flops 256 | bytes 2048
  22.6 27.6 %all-gather.2.cloned.1.call-done = bf16[1,128,7168]{2,1,0:T(8,128)(2,1)} async-done(((bf16[1,8,7168]{2,1,0:T(8,128)(2,1)}), bf16[1,128,7168]{2,1,0:T(8,128)(2,1)}) %all-gather.2.cloned.1.call-update) | async-done | bytes 1835024 | tf_op jit(solution)/shard_map/all_gather | solution.py:22
  50.3 0.0 copy-start.1
  50.3 1.4 collective-permute-start.1
  51.7 7.9 %fusion.10 = (f32[128]{0:T(128)S(1)}, f32[128,1010]{0,1:T(8,128)S(1)}) fusion(bf16[1010,7168]{1,0:T(8,128)(2,1)} %param.5, bf16[1,128,7168]{2,1,0:T(8,128)(2,1)} %all-gather.2.cloned.1.call-done), kind=kOutput, calls=%fused_computation.25 | convolution fusion | flops 1853487232 | bytes 16832000 | tf_op jit(solution)/shard_map/dot_general | solution.py:31
  59.6 30.5 %pmax.7 = f32[128]{0:T(128)S(1)} all-reduce(f32[128]{0:T(128)S(1)} %get-tuple-element.17), channel_id=1, replica_groups=mesh['seq'=2,'depth'=2,'vocab'=8] {'seq','vocab'}, use_global_device_ids=true, to_apply=%region_1.2 | all-reduce | flops 128 | bytes 1024 | tf_op jit(solution)/shard_map/pmax | solution.py:38
  90.2 0.2 fusion
  90.4 32.7 %all-reduce.3 = (f32[128]{0:T(128)S(1)}, f32[128]{0:T(128)S(1)}) all-reduce(f32[128]{0:T(128)S(1)} %get-tuple-element.8, f32[128]{0:T(128)S(1)} %get-tuple-element.7), channel_id=1, replica_groups=mesh['seq'=2,'depth'=2,'vocab'=8] {'seq','vocab'}, use_global_device_ids=true, to_apply=%region_3.4 | all-reduce | flops 256 | bytes 2048 | tf_op jit(solution)/shard_map/psum | solution.py:39
  123.1 0.6 fusion.5
  124.5 0.2 fusion.3
  124.7 0.8 collective-permute-start
  125.5 0.0 copy-done.1
  125.5 5.0 %convolution_convert_fusion.1 = bf16[505,7168]{1,0:T(8,128)(2,1)} fusion(bf16[128,1010]{0,1:T(8,128)(2,1)S(1)} %fusion.3, s32[]{:T(128)S(6)} %select_n.20, bf16[1,128,7168]{2,1,0:T(8,128)(2,1)S(1)} %copy-done.1), kind=kOutput, calls=%fused_computation.2 | convolution fusion | flops 930298880 | bytes 9205764 | tf_op jit(solution)/shard_map/dot_general | solution.py:14
  131.2 0.0 copy-start
  131.2 0.0 collective-permute-done
  131.2 0.0 collective-permute-done.1
  131.2 6.7 %convolution_convert_fusion = bf16[505,7168]{1,0:T(8,128)(2,1)} fusion(bf16[128,505]{0,1:T(8,128)(2,1)S(1)} %collective-permute-done, bf16[128,7168]{1,0:T(8,128)(2,1)} %collective-permute-done.1), kind=kOutput, calls=%fused_computation.1 | convolution fusion | flops 930298880 | bytes 9203968 | tf_op jit(solution)/shard_map/dot_general | solution.py:14
  138.0 0.0 copy-done
  138.0 7.5 %multiply_reduce_fusion = f32[]{:T(128)} fusion(bf16[505,7168]{1,0:T(8,128)(2,1)} %convolution_convert_fusion, bf16[505,7168]{1,0:T(8,128)(2,1)S(1)} %copy-done), kind=kLoop, calls=%fused_computation | loop fusion | flops 18099200 | bytes 14479364 | tf_op jit(solution)/shard_map/reduce_sum | solution.py:59
  145.4 0.6 dynamic-slice_bitcast_fusion
  146.0 5.4 %psum.30 = f32[]{:T(128)} all-reduce(f32[]{:T(128)S(6)} %mul.48), channel_id=1, replica_groups=mesh['seq'=2,'depth'=2,'vocab'=8] {'depth'}, use_global_device_ids=true, to_apply=%region_8.9 | all-reduce | flops 1 | bytes 8 | tf_op jit(solution)/shard_map/psum | solution.py:47
  151.4 42.0 %psum.31 = f32[]{:T(128)} all-reduce(f32[]{:T(128)} %multiply_reduce_fusion), channel_id=1, replica_groups=mesh['seq'=2,'depth'=2,'vocab'=8] {'seq','depth','vocab'}, use_global_device_ids=true, to_apply=%region_10.11 | all-reduce | flops 1 | bytes 8 | tf_op jit(solution)/shard_map/psum | solution.py:60
  (5 shorter events, 0.1 us)
Async XLA Ops:
  7.2 43.1 %all-gather.2.cloned.1.call-start = ((), (), s32[]{:S(2)}) async-start(), calls=%async_computation | async-start | bytes 1949696 | tf_op jit(solution)/shard_map/all_gather | solution.py:22
  50.3 75.2 %copy-start.1 = (bf16[1,128,7168]{2,1,0:T(8,128)(2,1)S(1)}, bf16[1,128,7168]{2,1,0:T(8,128)(2,1)}, u32[]{:S(2)}) copy-start(bf16[1,128,7168]{2,1,0:T(8,128)(2,1)} %all-gather.2.cloned.1.call-done) | copy-start | bytes 5505028
  50.3 81.0 %collective-permute-start.1 = (bf16[128,7168]{1,0:T(8,128)(2,1)}, bf16[128,7168]{1,0:T(8,128)(2,1)}, u32[]{:S(2)}, u32[]{:S(2)}) collective-permute-start(bf16[128,7168]{1,0:T(8,128)(2,1)} %bitcast.17), channel_id=1, source_target_pairs={{0,8},{8,0},{1,9},{9,1},{2,10},{10,2},{3,11},{11,3},{4,12},{12,4},... | collective-permute-start | bytes 5505032 | tf_op jit(solution)/shard_map/ppermute | solution.py:10
  124.7 6.5 %collective-permute-start = (bf16[128,505]{0,1:T(8,128)(2,1)S(1)}, bf16[128,505]{0,1:T(8,128)(2,1)S(1)}, u32[]{:S(2)}, u32[]{:S(2)}) collective-permute-start(bf16[128,505]{0,1:T(8,128)(2,1)S(1)} %constant_dynamic-slice_fusion), channel_id=1, source_target_pairs={{0,8},{8,0},{1,9},{9,1},{2,10},{10,2},{3,11},{11,3},{4,12},{12,4},... | collective-permute-start | bytes 387848 | tf_op jit(solution)/shard_map/ppermute | solution.py:10
  131.2 6.8 %copy-start = (bf16[505,7168]{1,0:T(8,128)(2,1)S(1)}, bf16[505,7168]{1,0:T(8,128)(2,1)}, u32[]{:S(2)}) copy-start(bf16[505,7168]{1,0:T(8,128)(2,1)} %convolution_convert_fusion.1) | copy-start | bytes 21719044
Sparse Core Ops, SparseCore 0:
  10.2 40.0 all-gather.1
where the time goes:
time: 203 us; the launch traced here: 202 us
  blocking collectives  122 us (60%)
  waiting for transfers between devices  28.3 us (14%)
  matrix products  19.7 us (10%)
  between operations  17.9 us (9%)
  other arithmetic  8.51 us (4%)
  local copies, waits for them, and re-layouts  3.37 us (2%)
  starting transfers between devices  2.28 us (1%)
    psum x1, blocking collectives, local(): grad_norm = jnp.sqrt(lax.psum(square, ('seq', 'depth', 'vocab')))  42 us
    psum x1, blocking collectives, local(): lax.psum((jnp.sum(jnp.exp(logits - peak[:, None]), axis=1), chosen), ('se...  32.7 us
    pmax x1, blocking collectives, local(): peak = lax.pmax(local_peak, ('seq', 'vocab'))  30.5 us
    all_gather x1, waiting for transfers between devices, local(): lax.all_gather(hidden, ('seq', 'vocab'), axis=1, tiled=True)  27.6 us
    dot_general x2, matrix products, rows_product(): lax.dot_general(grad_rows, states, (((0,), (0,)), ((), ())), preferred_el...  11.8 us
    unnamed x1, blocking collectives  11.3 us
    dot_general x1, matrix products, local(): lax.dot_general(states, embedding, (((1,), (1,)), ((), ())), preferred_el...  7.92 us
    reduce_sum x1, other arithmetic, local(): square = jnp.sum(summed * summed)  7.46 us
  transfers between devices with their start and end apart: 3, of which 1 were waited for; matrix products, arithmetic and copies ran while one was open for 8% of the time, Pallas kernels for 0%

commit v1 on v0

--- a/solution.py
+++ b/solution.py
@@ -37,7 +37,7 @@
     chosen = jnp.sum(jnp.where(onehot, logits, jnp.zeros((), jnp.float32)), axis=1)
     peak = lax.pmax(local_peak, ("seq", "vocab"))
     total, target = lax.psum(
-        (jnp.sum(jnp.exp(logits - peak[:, None]), axis=1), chosen), ("seq", "vocab")
+        lax.psum((jnp.sum(jnp.exp(logits - peak[:, None]), axis=1), chosen), "vocab"), "seq"
     )
     lse = peak + jnp.log(total)
     nll = lse - target

time: 203 us -> 192 us (0.946)
  blocking collectives: 122 us -> 112 us
    psum x1 -> x2, blocking collectives: 32.7 us -> 21.6 us  [the longest x1 19.2 us: local(): lax.psum((jnp.sum(jnp.exp(logits - peak[:, None]), axis=1), chosen), 'voc...]
  transfers between devices with their start and end apart: 3 -> 3, of which waited for: 1 -> 1; matrix products, arithmetic and copies ran while one was open for 8% -> 9% of each run, Pallas kernels for 0% -> 0%
where the time goes in v1:
time: 192 us
  blocking collectives  112 us (58%)
  waiting for transfers between devices  28.3 us (15%)
  matrix products  19.7 us (10%)
  between operations  17.9 us (9%)
  other arithmetic  8.51 us (4%)
  local copies, waits for them, and re-layouts  3.37 us (2%)
  starting transfers between devices  2.27 us (1%)
    psum x1, blocking collectives, local(): grad_norm = jnp.sqrt(lax.psum(square, ('seq', 'depth', 'vocab')))  42.9 us
    pmax x1, blocking collectives, local(): peak = lax.pmax(local_peak, ('seq', 'vocab'))  30.5 us
    all_gather x1, waiting for transfers between devices, local(): lax.all_gather(hidden, ('seq', 'vocab'), axis=1, tiled=True)  27.6 us
    psum x1, blocking collectives, local(): lax.psum((jnp.sum(jnp.exp(logits - peak[:, None]), axis=1), chosen), 'voc...  19.2 us
    dot_general x2, matrix products, rows_product(): lax.dot_general(grad_rows, states, (((0,), (0,)), ((), ())), preferred_el...  11.8 us
    unnamed x1, blocking collectives  11.3 us
    dot_general x1, matrix products, local(): lax.dot_general(states, embedding, (((1,), (1,)), ((), ())), preferred_el...  7.92 us
    reduce_sum x1, other arithmetic, local(): square = jnp.sum(summed * summed)  7.46 us
  transfers between devices with their start and end apart: 3, of which 1 were waited for; matrix products, arithmetic and copies ran while one was open for 9% of the time, Pallas kernels for 0%

profile of v1, /device:TPU:12, one launch (start us, length us, event | category | flops | bytes accessed | tf_op | source)
XLA Modules:
  0.0 191.9 jit_solution(8002323598386977825)
XLA Ops:
  7.2 0.0 all-gather.2.cloned.1.call-start
  7.2 0.7 all-gather.2.cloned.1.call-update
  7.9 1.2 dynamic-slice
  9.8 0.8 bitcast_dynamic-update-slice_fusion.1
  10.6 0.7 bitcast_dynamic-update-slice_fusion
  11.3 11.3 %all-reduce.2 = (s32[128]{0:T(128)S(1)}, s32[128]{0:T(128)S(1)}) all-reduce(s32[128]{0:T(128)S(1)} %bitcast_dynamic-update-slice_fusion.1, s32[128]{0:T(128)S(1)} %bitcast_dynamic-update-slice_fusion), channel_id=1, replica_groups=mesh['seq'=2,'depth'=2,'vocab'=8] {'seq','vocab'}, use_global_device_ids=true, to_apply=%add | all-reduce | flops 256 | bytes 2048
  22.6 27.6 %all-gather.2.cloned.1.call-done = bf16[1,128,7168]{2,1,0:T(8,128)(2,1)} async-done(((bf16[1,8,7168]{2,1,0:T(8,128)(2,1)}), bf16[1,128,7168]{2,1,0:T(8,128)(2,1)}) %all-gather.2.cloned.1.call-update) | async-done | bytes 1835024 | tf_op jit(solution)/shard_map/all_gather | solution.py:22
  50.3 0.0 copy-start.1
  50.3 1.4 collective-permute-start.1
  51.7 7.9 %fusion.10 = (f32[128]{0:T(128)S(1)}, f32[128,1010]{0,1:T(8,128)S(1)}) fusion(bf16[1010,7168]{1,0:T(8,128)(2,1)} %param.5, bf16[1,128,7168]{2,1,0:T(8,128)(2,1)} %all-gather.2.cloned.1.call-done), kind=kOutput, calls=%fused_computation.25 | convolution fusion | flops 1853487232 | bytes 16832000 | tf_op jit(solution)/shard_map/dot_general | solution.py:31
  59.6 30.5 %pmax.7 = f32[128]{0:T(128)S(1)} all-reduce(f32[128]{0:T(128)S(1)} %get-tuple-element.19), channel_id=1, replica_groups=mesh['seq'=2,'depth'=2,'vocab'=8] {'seq','vocab'}, use_global_device_ids=true, to_apply=%region_1.2 | all-reduce | flops 128 | bytes 1024 | tf_op jit(solution)/shard_map/pmax | solution.py:38
  90.2 0.2 fusion
  90.4 19.2 %all-reduce.3 = (f32[128]{0:T(128)S(1)}, f32[128]{0:T(128)S(1)}) all-reduce(f32[128]{0:T(128)S(1)} %get-tuple-element.8, f32[128]{0:T(128)S(1)} %get-tuple-element.7), channel_id=1, replica_groups=mesh['seq'=2,'depth'=2,'vocab'=8] {'vocab'}, use_global_device_ids=true, to_apply=%region_3.4 | all-reduce | flops 256 | bytes 2048 | tf_op jit(solution)/shard_map/psum | solution.py:40
  109.6 2.5 %all-reduce.4 = (f32[128]{0:T(128)S(1)}, f32[128]{0:T(128)S(1)}) all-reduce(f32[128]{0:T(128)S(1)} %get-tuple-element.13, f32[128]{0:T(128)S(1)} %get-tuple-element.14), channel_id=1, replica_groups=mesh['seq'=2,'depth'=2,'vocab'=8] {'seq'}, use_global_device_ids=true, to_apply=%region_4.5 | all-reduce | flops 256 | bytes 2048 | tf_op jit(solution)/shard_map/psum | solution.py:39
  112.1 0.6 fusion.5
  113.4 0.2 fusion.3
  113.7 0.8 collective-permute-start
  114.4 0.0 copy-done.1
  114.4 5.0 %convolution_convert_fusion.1 = bf16[505,7168]{1,0:T(8,128)(2,1)} fusion(bf16[128,1010]{0,1:T(8,128)(2,1)S(1)} %fusion.3, s32[]{:T(128)S(6)} %select_n.20, bf16[1,128,7168]{2,1,0:T(8,128)(2,1)S(1)} %copy-done.1), kind=kOutput, calls=%fused_computation.2 | convolution fusion | flops 930298880 | bytes 9205764 | tf_op jit(solution)/shard_map/dot_general | solution.py:14
  120.1 0.0 copy-start
  120.1 0.0 collective-permute-done
  120.2 0.0 collective-permute-done.1
  120.2 6.7 %convolution_convert_fusion = bf16[505,7168]{1,0:T(8,128)(2,1)} fusion(bf16[128,505]{0,1:T(8,128)(2,1)S(1)} %collective-permute-done, bf16[128,7168]{1,0:T(8,128)(2,1)} %collective-permute-done.1), kind=kOutput, calls=%fused_computation.1 | convolution fusion | flops 930298880 | bytes 9203968 | tf_op jit(solution)/shard_map/dot_general | solution.py:14
  126.9 0.0 copy-done
  126.9 7.5 %multiply_reduce_fusion = f32[]{:T(128)} fusion(bf16[505,7168]{1,0:T(8,128)(2,1)} %convolution_convert_fusion, bf16[505,7168]{1,0:T(8,128)(2,1)S(1)} %copy-done), kind=kLoop, calls=%fused_computation | loop fusion | flops 18099200 | bytes 14479364 | tf_op jit(solution)/shard_map/reduce_sum | solution.py:59
  134.4 0.6 dynamic-slice_bitcast_fusion
  135.0 5.4 %psum.46 = f32[]{:T(128)} all-reduce(f32[]{:T(128)S(6)} %mul.48), channel_id=1, replica_groups=mesh['seq'=2,'depth'=2,'vocab'=8] {'depth'}, use_global_device_ids=true, to_apply=%region_10.11 | all-reduce | flops 1 | bytes 8 | tf_op jit(solution)/shard_map/psum | solution.py:47
  140.4 42.9 %psum.47 = f32[]{:T(128)} all-reduce(f32[]{:T(128)} %multiply_reduce_fusion), channel_id=1, replica_groups=mesh['seq'=2,'depth'=2,'vocab'=8] {'seq','depth','vocab'}, use_global_device_ids=true, to_apply=%region_12.13 | all-reduce | flops 1 | bytes 8 | tf_op jit(solution)/shard_map/psum | solution.py:60
  (5 shorter events, 0.1 us)
Async XLA Ops:
  7.2 43.1 %all-gather.2.cloned.1.call-start = ((), (), s32[]{:S(2)}) async-start(), calls=%async_computation | async-start | bytes 1949696 | tf_op jit(solution)/shard_map/all_gather | solution.py:22
  50.3 64.2 %copy-start.1 = (bf16[1,128,7168]{2,1,0:T(8,128)(2,1)S(1)}, bf16[1,128,7168]{2,1,0:T(8,128)(2,1)}, u32[]{:S(2)}) copy-start(bf16[1,128,7168]{2,1,0:T(8,128)(2,1)} %all-gather.2.cloned.1.call-done) | copy-start | bytes 5505028
  50.3 69.9 %collective-permute-start.1 = (bf16[128,7168]{1,0:T(8,128)(2,1)}, bf16[128,7168]{1,0:T(8,128)(2,1)}, u32[]{:S(2)}, u32[]{:S(2)}) collective-permute-start(bf16[128,7168]{1,0:T(8,128)(2,1)} %bitcast.17), channel_id=1, source_target_pairs={{0,8},{8,0},{1,9},{9,1},{2,10},{10,2},{3,11},{11,3},{4,12},{12,4},... | collective-permute-start | bytes 5505032 | tf_op jit(solution)/shard_map/ppermute | solution.py:10
  113.7 6.5 %collective-permute-start = (bf16[128,505]{0,1:T(8,128)(2,1)S(1)}, bf16[128,505]{0,1:T(8,128)(2,1)S(1)}, u32[]{:S(2)}, u32[]{:S(2)}) collective-permute-start(bf16[128,505]{0,1:T(8,128)(2,1)S(1)} %constant_dynamic-slice_fusion), channel_id=1, source_target_pairs={{0,8},{8,0},{1,9},{9,1},{2,10},{10,2},{3,11},{11,3},{4,12},{12,4},... | collective-permute-start | bytes 387848 | tf_op jit(solution)/shard_map/ppermute | solution.py:10
  120.1 6.8 %copy-start = (bf16[505,7168]{1,0:T(8,128)(2,1)S(1)}, bf16[505,7168]{1,0:T(8,128)(2,1)}, u32[]{:S(2)}) copy-start(bf16[505,7168]{1,0:T(8,128)(2,1)} %convolution_convert_fusion.1) | copy-start | bytes 21719044
Sparse Core Ops, SparseCore 0:
  10.2 40.0 all-gather.1
